TPU v7x, 32 devices: a whole 2x2x4 slice. The times are simulated.
32 devices in a mesh: pipe: 4 (over x, core), expert: 4 (over z), tensor: 2 (over y).
Axes of the slice: x: 2, y: 2, z: 4, core: 2. Of those that a mesh axis runs over, the one named last changes fastest.
Arguments:
- stream: bfloat16 [2, 4, 64, 7168], P(None, 'pipe', 'expert', 'tensor'), may hold values from -6 to 6
- expert_ids: int32 [2, 4, 64, 2], P(None, 'pipe', 'expert'), may hold values from 0 to 3, all different within a row; in each aligned block of 16 rows (0 to 15, 16 to 31, ..., all dimensions but the last counted through in order) at most 12 rows name the same one
- norm_gain: float32 [4, 7168], P('pipe', 'tensor'), may hold values from 0.1 to 1.9
- router: float32 [4, 7168, 4], P('pipe', 'tensor'), may hold values from -0.0625 to 0.0625
- w_up: bfloat16 [4, 7168, 1024], P('expert', 'tensor'), may hold values from -0.0625 to 0.0625
- w_down: bfloat16 [4, 1024, 7168], P('expert', None, 'tensor'), may hold values from -0.1875 to 0.1875
Outputs:
- result: bfloat16 [2, 4, 64, 7168], P(None, 'pipe', 'expert', 'tensor')
Inputs may be any that keep to these rules, and one draw needn't show every extreme that they name: `expert_ids`: each token names 2 different experts. Among the 16 tokens of one direction held by one index of the expert axis at one section, at most 12 name any one expert, and in every draw some expert is named by exactly 12 of them.
All inputs are finite; a program needn't handle non-finite values.
Results may differ from a plain program's by a relative error of at most 0.0065.
Values may be sent and summed in bfloat16 or wider, within the bound.
A program may use at most 64 MiB of HBM per device.

v0:
```python
import jax
import jax.numpy as jnp
from jax import lax
from jax.sharding import PartitionSpec as P

norm_eps = 1e-06
route_scale = 2.5


def shifted(x, axis, by):
    size = lax.axis_size(axis)
    return lax.ppermute(x, axis, [(i, (i + by) % size) for i in range(size)])


def shards(stream, expert_ids, norm_gain, router, w_up, w_down):
    ahead = shifted(stream[0], "pipe", 1)
    behind = shifted(stream[1], "pipe", -1)
    arrived = jnp.concatenate([ahead, behind], axis=0).astype(jnp.float32)
    tok_rows = arrived.shape[1]
    quarter = arrived.shape[2]
    width = float(quarter * lax.axis_size("tensor"))
    scaled = arrived * norm_gain[0]
    squares = jnp.sum(arrived * arrived, axis=-1)
    highest = lax.Precision.HIGHEST
    total_sq = lax.psum(squares, "tensor")
    inverse = lax.rsqrt(total_sq / width + norm_eps)
    normed = scaled * inverse[..., None]
    logits = lax.psum(jnp.einsum("dtc,ce->dte", normed, router[0], precision=highest), "tensor")
    chosen = expert_ids[:, 0]
    fanout = chosen.shape[2]
    experts = router.shape[2]
    capacity = 3 * tok_rows * fanout // (2 * experts)
    picked = jnp.take_along_axis(logits, chosen, axis=-1)
    scores = jax.nn.sigmoid(picked)
    gates = route_scale * scores / jnp.sum(scores, axis=-1, keepdims=True)
    onehot = (chosen[..., None] == jnp.arange(experts, dtype=jnp.int32)).astype(jnp.int32)
    onehot = onehot.reshape(2, tok_rows * fanout, experts)
    earlier = jnp.cumsum(onehot, axis=1) - onehot
    within = jnp.sum(earlier * onehot, axis=-1).reshape(chosen.shape)
    heading = lax.broadcasted_iota(jnp.int32, chosen.shape, 0)
    member = lax.broadcasted_iota(jnp.int32, chosen.shape, 1)
    target = chosen * (2 * capacity) + heading * capacity + within
    anchor = heading * tok_rows + member
    owner = (
        jnp.full((experts * 2 * capacity,), 2 * tok_rows, jnp.int32)
        .at[target.reshape(-1)]
        .set(anchor.reshape(-1))
    )
    hidden = normed.astype(jnp.bfloat16).reshape(2 * tok_rows, quarter)
    table = jnp.concatenate([hidden, jnp.zeros((1, quarter), jnp.bfloat16)], axis=0)
    outgoing = table[owner].reshape(experts, 2 * capacity, quarter)
    upper = w_up[0]
    lower = w_down[0]
    received = lax.all_to_all(outgoing, "expert", split_axis=0, concat_axis=0, tiled=True)
    senders = received.shape[0]
    count = received.shape[1]
    inner = jnp.dot(received.reshape(-1, quarter), upper, preferred_element_type=jnp.float32)
    share = lax.psum_scatter(inner, "tensor", scatter_dimension=1, tiled=True)
    active = lax.all_gather(jax.nn.silu(share).astype(jnp.bfloat16), "tensor", axis=1, tiled=True)
    produced = jnp.dot(active, lower, preferred_element_type=jnp.float32).astype(jnp.bfloat16)
    answers = lax.all_to_all(
        produced.reshape(senders, count, quarter), "expert", split_axis=0, concat_axis=0, tiled=True
    )
    flat_back = answers.reshape(experts * 2 * capacity, quarter)
    gathered = (
        flat_back[target.reshape(-1)].reshape(2, tok_rows, fanout, quarter).astype(jnp.float32)
    )
    mixed = jnp.einsum("dtk,dtkc->dtc", gates, gathered)
    result = (arrived + mixed).astype(jnp.bfloat16)
    return result[:, None]


def solution(mesh):
    return jax.shard_map(
        shards,
        mesh=mesh,
        in_specs=(
            P(None, "pipe", "expert", "tensor"),
            P(None, "pipe", "expert", None),
            P("pipe", "tensor"),
            P("pipe", "tensor", None),
            P("expert", "tensor", None),
            P("expert", None, "tensor"),
        ),
        out_specs=P(None, "pipe", "expert", "tensor"),
        check_vma=False,
    )
```

profile of v0, /device:TPU:0, one launch (start us, length us, event | category | flops | bytes accessed | tf_op | source)
XLA Modules:
  0.0 101.9 jit_solution(15306226972587400173)
XLA Ops:
  6.5 0.0 copy-start
  6.5 1.0 slice_bitcast_fusion.1
  7.5 0.5 collective-permute-start
  8.1 2.0 %collective-permute-start.1 = (bf16[1,16,3584]{2,1,0:T(8,128)(2,1)S(1)}, bf16[1,16,3584]{2,1,0:T(8,128)(2,1)S(1)}, u32[]{:S(2)}, u32[]{:S(2)}) collective-permute-start(bf16[1,16,3584]{2,1,0:T(8,128)(2,1)S(1)} %get-tuple-element.8), channel_id=1, source_target_pairs={{0,24},{8,0},{16,8},{24,16},{1,25},{9,1},{17,9},{25,17},{2,26},{10... | collective-permute-start | bytes 344072 | tf_op jit(solution)/shard_map/ppermute | solution.py:12
  10.0 0.8 copy.14
  10.8 0.7 broadcast_multiply_fusion
  11.5 0.1 eq.16
  11.6 0.1 fusion.18
  11.7 0.1 reduce_window_sum.11
  11.7 0.2 select_reduce_fusion
  11.9 0.1 reshape.116
  12.0 0.1 copy.13
  12.1 0.1 mul.92
  12.2 0.1 iota.24
  12.3 0.1 iota.25
  12.4 0.1 iota_add_fusion
  12.5 0.1 reshape.149
  12.6 0.8 scatter_custom_fusion
  13.4 0.8 reduce
  14.1 0.0 collective-permute-done
  14.2 0.0 collective-permute-done.1
  14.2 0.1 multiply_reduce_fusion
  14.3 5.2 %psum.14 = f32[2,16]{1,0:T(2,128)S(1)} all-reduce(f32[2,16]{1,0:T(2,128)S(1)} %multiply_reduce_fusion), channel_id=1, replica_groups=mesh['pipe'=4,'expert'=4,'tensor'=2] {'tensor'}, use_global_device_ids=true, to_apply=%region_1.0 | all-reduce | flops 32 | bytes 256 | tf_op jit(solution)/shard_map/psum | solution.py:25
  19.5 0.1 mul.87
  19.6 0.1 fusion.9
  19.7 1.0 gather_fusion
  20.7 22.2 %all_to_all.10 = bf16[4,24,3584]{2,1,0:T(8,128)(2,1)S(1)} all-to-all(bf16[4,24,3584]{2,1,0:T(8,128)(2,1)S(1)} %bitcast.63), channel_id=1, replica_groups=mesh['pipe'=4,'expert'=4,'tensor'=2] {'expert'}, dimensions={0} | all-to-all | bytes 1376256 | tf_op jit(solution)/shard_map/all_to_all | solution.py:54
  42.8 5.1 %fusion.2 = f32[96,1024]{1,0:T(8,128)} fusion(bf16[96,3584]{1,0:T(8,128)(2,1)S(1)} %bitcast.62, bf16[1,3584,1024]{2,1,0:T(8,128)(2,1)} %param.10), kind=kOutput, calls=%fused_computation.6 | convolution fusion | flops 704643072 | bytes 8421376 | tf_op jit(solution)/shard_map/dot_general | solution.py:57
  47.9 0.0 reduce-scatter.2.cloned.1.call-update
  48.0 11.9 %reduce-scatter.2.cloned.1.call-done = f32[96,512]{1,0:T(8,128)} async-done(((f32[96,1024]{1,0:T(8,128)}), f32[96,512]{1,0:T(8,128)}) %reduce-scatter.2.cloned.1.call-update) | async-done | bytes 196624 | tf_op jit(solution)/shard_map/reduce_scatter | solution.py:58
  59.9 1.0 multiply_convert_fusion
  60.9 5.3 %all_gather.3 = bf16[96,1024]{1,0:T(8,128)(2,1)S(1)} all-gather(bf16[96,512]{1,0:T(8,128)(2,1)S(1)} %multiply_convert_fusion), channel_id=1, replica_groups=mesh['pipe'=4,'expert'=4,'tensor'=2] {'tensor'}, dimensions={1}, use_global_device_ids=true | all-gather | bytes 294912 | tf_op jit(solution)/shard_map/all_gather | solution.py:59
  66.2 5.2 %fusion.4 = bf16[96,3584]{1,0:T(8,128)(2,1)} fusion(bf16[96,1024]{1,0:T(8,128)(2,1)S(1)} %all_gather.3, bf16[1,1024,3584]{2,1,0:T(8,128)(2,1)} %param.11), kind=kOutput, calls=%fused_computation.8 | convolution fusion | flops 704987136 | bytes 8224768 | tf_op jit(solution)/shard_map/dot_general | solution.py:60
  71.4 4.6 %all-to-all-start.1 = ((bf16[4,24,3584]{2,1,0:T(8,128)(2,1)}), bf16[4,24,3584]{2,1,0:T(8,128)(2,1)S(1)}, u32[]{:S(2)}, u32[]{:S(2)}) async-start(bf16[4,24,3584]{2,1,0:T(8,128)(2,1)} %bitcast.13), calls=%async_computation.2 | async-start | bytes 1376256 | tf_op jit(solution)/shard_map/all_to_all | solution.py:61
  76.0 0.0 copy-done.1
  76.0 0.1 copy.11
  76.1 0.1 reshape.139
  76.2 1.8 %fusion.10 = f32[2,16,4]{1,2,0:T(4,128)S(1)} fusion(f32[2,16]{1,0:T(2,128)S(1)} %add_rsqrt_fusion, f32[3584]{0:T(1024)S(1)} %reduce, f32[1,3584,4]{1,2,0:T(4,128)S(1)} %copy-done, bf16[1,16,3584]{2,1,0:T(8,128)(2,1)S(1)} %collective-permute-done.1, bf16[1,16,3584]{2,1,0:T(8,128)(2,1)S(1)} %collective-permute-done), kind=kOutput, calls=%fused_computation.14 | convolution fusion | flops 5963776 | bytes 301696 | tf_op jit(solution)/shard_map/dtc,ce->dte/dot_general | solution.py:28
  78.0 4.9 %psum.15 = f32[2,16,4]{1,2,0:T(4,128)S(1)} all-reduce(f32[2,16,4]{1,2,0:T(4,128)S(1)} %fusion.10), channel_id=1, replica_groups=mesh['pipe'=4,'expert'=4,'tensor'=2] {'tensor'}, use_global_device_ids=true, to_apply=%region_2.0 | all-reduce | flops 128 | bytes 1024 | tf_op jit(solution)/shard_map/psum | solution.py:28
  82.9 1.0 gather_fusion.2
  83.9 0.1 reshape.142
  84.0 0.1 copy.12
  84.2 0.1 copy.15
  84.3 8.4 %all-to-all-done.1 = bf16[4,24,3584]{2,1,0:T(8,128)(2,1)S(1)} async-done(((bf16[4,24,3584]{2,1,0:T(8,128)(2,1)}), bf16[4,24,3584]{2,1,0:T(8,128)(2,1)S(1)}, u32[]{:S(2)}, u32[]{:S(2)}) %all-to-all-start.1) | async-done | bytes 688160 | tf_op jit(solution)/shard_map/all_to_all | solution.py:61
  92.7 0.8 gather_fusion.1
  93.5 0.2 reshape.121
  93.7 0.6 fusion.27
  94.3 0.7 fusion.14
  (14 shorter events, 0.1 us)
Async XLA Ops:
  6.5 69.7 %copy-start = (f32[1,3584,4]{1,2,0:T(4,128)S(1)}, f32[1,3584,4]{1,2,0:T(4,128)}, u32[]{:S(2)}) copy-start(f32[1,3584,4]{1,2,0:T(4,128)} %param.9) | copy-start | bytes 172036
  6.5 53.3 %reduce-scatter.2.cloned.1.call-start = ((), (), s32[]{:S(2)}) async-start(), calls=%async_computation.3 | async-start | bytes 589824 | tf_op jit(solution)/shard_map/reduce_scatter | solution.py:58
  7.5 6.6 %collective-permute-start = (bf16[1,16,3584]{2,1,0:T(8,128)(2,1)S(1)}, bf16[1,16,3584]{2,1,0:T(8,128)(2,1)S(1)}, u32[]{:S(2)}, u32[]{:S(2)}) collective-permute-start(bf16[1,16,3584]{2,1,0:T(8,128)(2,1)S(1)} %get-tuple-element.7), channel_id=1, source_target_pairs={{0,8},{8,16},{16,24},{24,0},{1,9},{9,17},{17,25},{25,1},{2,10},{10... | collective-permute-start | bytes 344072 | tf_op jit(solution)/shard_map/ppermute | solution.py:12
  8.1 6.1 %collective-permute-start.1 = (bf16[1,16,3584]{2,1,0:T(8,128)(2,1)S(1)}, bf16[1,16,3584]{2,1,0:T(8,128)(2,1)S(1)}, u32[]{:S(2)}, u32[]{:S(2)}) collective-permute-start(bf16[1,16,3584]{2,1,0:T(8,128)(2,1)S(1)} %get-tuple-element.8), channel_id=1, source_target_pairs={{0,24},{8,0},{16,8},{24,16},{1,25},{9,1},{17,9},{25,17},{2,26},{10... | collective-permute-start | bytes 344072 | tf_op jit(solution)/shard_map/ppermute | solution.py:12
  66.1 9.9 %copy-start.1 = (s32[2,1,16,2]{2,3,1,0:T(2,128)S(1)}, s32[2,1,16,2]{2,3,1,0:T(2,128)}, u32[]{:S(2)}) copy-start(s32[2,1,16,2]{2,3,1,0:T(2,128)} %param.7) | copy-start | bytes 772
  71.4 21.3 %all-to-all-start.1 = ((bf16[4,24,3584]{2,1,0:T(8,128)(2,1)}), bf16[4,24,3584]{2,1,0:T(8,128)(2,1)S(1)}, u32[]{:S(2)}, u32[]{:S(2)}) async-start(bf16[4,24,3584]{2,1,0:T(8,128)(2,1)} %bitcast.13), calls=%async_computation.2 | async-start | bytes 1376256 | tf_op jit(solution)/shard_map/all_to_all | solution.py:61
Sparse Core Ops, SparseCore 0:
  48.1 11.7 reduce-scatter.1
where the time goes:
time: 102 us
  blocking collectives  37.5 us (37%)
  waiting for transfers between devices  20.4 us (20%)
  between operations  13.6 us (13%)
  matrix products  12.8 us (13%)
  starting transfers between devices  7.13 us (7%)
  local copies, waits for them, and re-layouts  6.7 us (7%)
  other arithmetic  3.87 us (4%)
    all_to_all x1, blocking collectives, shards(): lax.all_to_all(outgoing, 'expert', split_axis=0, concat_axis=0, tiled=True)  22.2 us
    reduce_scatter x1, waiting for transfers between devices, shards(): share = lax.psum_scatter(inner, 'tensor', scatter_dimension=1, tiled=True)  11.9 us
    all_to_all x1, waiting for transfers between devices, shards(): lax.all_to_all(produced.reshape(senders, count, quarter), 'expert', split...  8.42 us
    all_gather x1, blocking collectives, shards(): lax.all_gather(jax.nn.silu(share).astype(jnp.bfloat16), 'tensor', axis=1,...  5.29 us
    dot_general x1, matrix products, shards(): jnp.dot(active, lower, preferred_element_type=jnp.float32)  5.25 us
    psum x1, blocking collectives, shards(): total_sq = lax.psum(squares, 'tensor')  5.16 us
    dot_general x1, matrix products, shards(): jnp.dot(received.reshape(-1, quarter), upper, preferred_element_type=jnp....  5.11 us
    psum x1, blocking collectives, shards(): lax.psum(jnp.einsum('dtc,ce->dte', normed, router[0], precision=highest),...  4.93 us
  transfers between devices with their start and end apart: 4, of which 2 were waited for; matrix products, arithmetic and copies ran while one was open for 7% of the time, Pallas kernels for 0%

commit v1 on v0

--- a/solution.py
+++ b/solution.py
@@ -58,9 +58,20 @@
     share = lax.psum_scatter(inner, "tensor", scatter_dimension=1, tiled=True)
     active = lax.all_gather(jax.nn.silu(share).astype(jnp.bfloat16), "tensor", axis=1, tiled=True)
     produced = jnp.dot(active, lower, preferred_element_type=jnp.float32).astype(jnp.bfloat16)
-    answers = lax.all_to_all(
-        produced.reshape(senders, count, quarter), "expert", split_axis=0, concat_axis=0, tiled=True
-    )
+    x_2 = produced.reshape(senders, count, quarter)
+    ways, here = (lax.axis_size("expert"), lax.axis_index("expert"))
+    width_2 = x_2.shape[0] // ways
+    lengths = list(x_2.shape)
+    lengths[0] = width_2
+    height = lengths[0]
+    lengths[0] = height * ways
+    full = jnp.zeros(lengths, x_2.dtype)
+    for mask in range(ways):
+        part = lax.dynamic_slice_in_dim(x_2, (here ^ mask) * width_2, width_2, axis=0)
+        if mask:
+            part = lax.ppermute(part, "expert", [(d, d ^ mask) for d in range(ways)])
+        full = lax.dynamic_update_slice_in_dim(full, part, (here ^ mask) * height, axis=0)
+    answers = full
     flat_back = answers.reshape(experts * 2 * capacity, quarter)
     gathered = (
         flat_back[target.reshape(-1)].reshape(2, tok_rows, fanout, quarter).astype(jnp.float32)

time: 102 us -> 98.1 us (0.962)
  blocking collectives: 37.5 us -> 15.1 us
  waiting for transfers between devices: 20.4 us -> 33.6 us
  starting transfers between devices: 7.13 us -> 11.9 us
    all_to_all x1 -> x0, blocking collectives: 22.2 us -> none  [shards(): lax.all_to_all(outgoing, 'expert', split_axis=0, concat_axis=0, tiled=True)]
    ppermute x0 -> x3, waiting for transfers between devices: none -> 11.6 us  [shards(): part = lax.ppermute(part, 'expert', [(d, d ^ mask) for d in range(ways)])]
    all_to_all x1, waiting for transfers between devices: 8.42 us -> 17.3 us  [shards(): lax.all_to_all(outgoing, 'expert', split_axis=0, concat_axis=0, tiled=True)]
    reduce_scatter x1, waiting for transfers between devices: 11.9 us -> 4.23 us  [shards(): share = lax.psum_scatter(inner, 'tensor', scatter_dimension=1, tiled=True)]
    ppermute x0 -> x3, starting transfers between devices: none -> 4.52 us  [shards(): part = lax.ppermute(part, 'expert', [(d, d ^ mask) for d in range(ways)])]
  transfers between devices with their start and end apart: 4 -> 7, of which waited for: 2 -> 5; matrix products, arithmetic and copies ran while one was open for 7% -> 8% of each run, Pallas kernels for 0% -> 0%
where the time goes in v1:
time: 98.1 us; the launch traced here: 97.7 us
  waiting for transfers between devices  33.6 us (34%)
  blocking collectives  15.1 us (15%)
  between operations  13.6 us (14%)
  starting transfers between devices  11.9 us (12%)
  matrix products  11.9 us (12%)
  local copies, waits for them, and re-layouts  7.72 us (8%)
  other arithmetic  3.87 us (4%)
    all_to_all x1, waiting for transfers between devices, shards(): lax.all_to_all(outgoing, 'expert', split_axis=0, concat_axis=0, tiled=True)  17.3 us
    ppermute x3, waiting for transfers between devices, shards(): part = lax.ppermute(part, 'expert', [(d, d ^ mask) for d in range(ways)])  11.6 us
    all_gather x1, blocking collectives, shards(): lax.all_gather(jax.nn.silu(share).astype(jnp.bfloat16), 'tensor', axis=1,...  5.29 us
    dot_general x1, matrix products, shards(): jnp.dot(received.reshape(-1, quarter), upper, preferred_element_type=jnp....  5.13 us
    psum x1, blocking collectives, shards(): lax.psum(jnp.einsum('dtc,ce->dte', normed, router[0], precision=highest),...  4.93 us
    psum x1, blocking collectives, shards(): total_sq = lax.psum(squares, 'tensor')  4.92 us
    all_to_all x1, starting transfers between devices, shards(): lax.all_to_all(outgoing, 'expert', split_axis=0, concat_axis=0, tiled=True)  4.87 us
    ppermute x3, starting transfers between devices, shards(): part = lax.ppermute(part, 'expert', [(d, d ^ mask) for d in range(ways)])  4.52 us
  transfers between devices with their start and end apart: 7, of which 5 were waited for; matrix products, arithmetic and copies ran while one was open for 8% of the time, Pallas kernels for 0%

profile of v1, /device:TPU:0, one launch (start us, length us, event | category | flops | bytes accessed | tf_op | source)
XLA Modules:
  0.0 97.7 jit_solution(7329529562692589962)
XLA Ops:
  6.5 1.0 slice_bitcast_fusion.1
  7.5 2.5 %collective-permute-start.1 = (bf16[1,16,3584]{2,1,0:T(8,128)(2,1)S(1)}, bf16[1,16,3584]{2,1,0:T(8,128)(2,1)S(1)}, u32[]{:S(2)}, u32[]{:S(2)}) collective-permute-start(bf16[1,16,3584]{2,1,0:T(8,128)(2,1)S(1)} %get-tuple-element.12), channel_id=1, source_target_pairs={{0,24},{8,0},{16,8},{24,16},{1,25},{9,1},{17,9},{25,17},{2,26},{10... | collective-permute-start | bytes 344072 | tf_op jit(solution)/shard_map/ppermute | solution.py:12
  10.0 0.8 copy.14
  10.7 0.7 broadcast_multiply_fusion
  11.4 0.1 eq.16
  11.5 0.1 fusion.18
  11.6 0.1 reduce_window_sum.11
  11.7 0.2 select_reduce_fusion
  11.8 0.1 reshape.116
  11.9 0.1 copy.13
  12.0 0.1 mul.92
  12.1 0.1 iota.24
  12.2 0.1 iota.25
  12.3 0.1 iota_add_fusion
  12.4 0.1 reshape.149
  12.5 0.8 scatter_custom_fusion
  13.3 0.8 reduce
  14.1 0.5 collective-permute-done
  14.5 0.1 multiply_reduce_fusion
  14.7 4.9 %psum.14 = f32[2,16]{1,0:T(2,128)S(1)} all-reduce(f32[2,16]{1,0:T(2,128)S(1)} %multiply_reduce_fusion), channel_id=1, replica_groups=mesh['pipe'=4,'expert'=4,'tensor'=2] {'tensor'}, use_global_device_ids=true, to_apply=%region_1.0 | all-reduce | flops 32 | bytes 256 | tf_op jit(solution)/shard_map/psum | solution.py:25
  19.6 0.1 mul.87
  19.7 0.1 fusion.9
  19.8 1.8 %gather_fusion = bf16[96,3584]{1,0:T(8,128)(2,1)} fusion(bf16[33,3584]{1,0:T(8,128)(2,1)S(1)} %concatenate.7, s32[1024]{0:T(1024)S(1)} %pad_clamp_fusion.1), kind=kCustom, calls=%fused_computation | custom fusion | bytes 1376640 | tf_op jit(solution)/shard_map/gather | solution.py:51
  21.6 4.9 %all-to-all-start = ((bf16[4,24,3584]{2,1,0:T(8,128)(2,1)}), bf16[4,24,3584]{2,1,0:T(8,128)(2,1)S(1)}, u32[]{:S(2)}, u32[]{:S(2)}) async-start(bf16[4,24,3584]{2,1,0:T(8,128)(2,1)} %bitcast.9), calls=%async_computation | async-start | bytes 1376256 | tf_op jit(solution)/shard_map/all_to_all | solution.py:54
  26.5 17.3 %all-to-all-done = bf16[4,24,3584]{2,1,0:T(8,128)(2,1)S(1)} async-done(((bf16[4,24,3584]{2,1,0:T(8,128)(2,1)}), bf16[4,24,3584]{2,1,0:T(8,128)(2,1)S(1)}, u32[]{:S(2)}, u32[]{:S(2)}) %all-to-all-start) | async-done | bytes 688160 | tf_op jit(solution)/shard_map/all_to_all | solution.py:54
  43.8 5.1 %fusion.2 = f32[96,1024]{1,0:T(8,128)} fusion(bf16[96,3584]{1,0:T(8,128)(2,1)S(1)} %bitcast.62, bf16[1,3584,1024]{2,1,0:T(8,128)(2,1)} %param.10), kind=kOutput, calls=%fused_computation.6 | convolution fusion | flops 704643072 | bytes 8421376 | tf_op jit(solution)/shard_map/dot_general | solution.py:57
  49.0 0.1 copy.11
  49.1 0.1 reshape.139
  49.2 1.8 %fusion.10 = f32[2,16,4]{1,2,0:T(4,128)S(1)} fusion(f32[2,16]{1,0:T(2,128)S(1)} %add_rsqrt_fusion, f32[3584]{0:T(1024)S(1)} %reduce, f32[1,3584,4]{1,2,0:T(4,128)S(1)} %copy-done, bf16[1,16,3584]{2,1,0:T(8,128)(2,1)S(1)} %collective-permute-done.1, bf16[1,16,3584]{2,1,0:T(8,128)(2,1)S(1)} %collective-permute-done), kind=kOutput, calls=%fused_computation.14 | convolution fusion | flops 5963776 | bytes 301696 | tf_op jit(solution)/shard_map/dtc,ce->dte/dot_general | solution.py:28
  51.0 4.9 %psum.15 = f32[2,16,4]{1,2,0:T(4,128)S(1)} all-reduce(f32[2,16,4]{1,2,0:T(4,128)S(1)} %fusion.10), channel_id=1, replica_groups=mesh['pipe'=4,'expert'=4,'tensor'=2] {'tensor'}, use_global_device_ids=true, to_apply=%region_2.0 | all-reduce | flops 128 | bytes 1024 | tf_op jit(solution)/shard_map/psum | solution.py:28
  55.9 1.0 gather_fusion.2
  56.9 0.1 reshape.142
  57.0 0.1 copy.12
  57.1 4.2 %reduce-scatter.2.cloned.1.call-done = f32[96,512]{1,0:T(8,128)} async-done(((f32[96,1024]{1,0:T(8,128)}), f32[96,512]{1,0:T(8,128)}) %reduce-scatter.2.cloned.1.call-update) | async-done | bytes 196624 | tf_op jit(solution)/shard_map/reduce_scatter | solution.py:58
  61.4 1.0 %multiply_convert_fusion = bf16[96,512]{1,0:T(8,128)(2,1)S(1)} fusion(f32[96,512]{1,0:T(8,128)} %reduce-scatter.2.cloned.1.call-done), kind=kLoop, calls=%fused_computation.23 | loop fusion | flops 245760 | bytes 294912 | tf_op jit(solution)/shard_map/convert_element_type | solution.py:59
  62.4 5.3 %all_gather.3 = bf16[96,1024]{1,0:T(8,128)(2,1)S(1)} all-gather(bf16[96,512]{1,0:T(8,128)(2,1)S(1)} %multiply_convert_fusion), channel_id=1, replica_groups=mesh['pipe'=4,'expert'=4,'tensor'=2] {'tensor'}, dimensions={1}, use_global_device_ids=true | all-gather | bytes 294912 | tf_op jit(solution)/shard_map/all_gather | solution.py:59
  67.6 4.4 %fusion.4 = bf16[96,3584]{1,0:T(8,128)(2,1)S(1)} fusion(bf16[96,1024]{1,0:T(8,128)(2,1)S(1)} %all_gather.3, bf16[1,1024,3584]{2,1,0:T(8,128)(2,1)} %param.11), kind=kOutput, calls=%fused_computation.8 | convolution fusion | flops 704987136 | bytes 8224768 | tf_op jit(solution)/shard_map/dot_general | solution.py:60
  72.1 0.1 constant_dynamic-slice_fusion.2
  72.1 1.5 %collective-permute-start.2 = (bf16[1,24,3584]{2,1,0:T(8,128)(2,1)S(1)}, bf16[1,24,3584]{2,1,0:T(8,128)(2,1)S(1)}, u32[]{:S(2)}, u32[]{:S(2)}) collective-permute-start(bf16[1,24,3584]{2,1,0:T(8,128)(2,1)S(1)} %get-tuple-element.9), channel_id=1, source_target_pairs={{0,2},{2,0},{4,6},{6,4},{1,3},{3,1},{5,7},{7,5},{8,10},{10,8},{12,... | collective-permute-start | bytes 516104 | tf_op jit(solution)/shard_map/ppermute | solution.py:72
  73.7 0.1 copy.15
  73.8 2.5 %collective-permute-start.3 = (bf16[1,24,3584]{2,1,0:T(8,128)(2,1)S(1)}, bf16[1,24,3584]{2,1,0:T(8,128)(2,1)S(1)}, u32[]{:S(2)}, u32[]{:S(2)}) collective-permute-start(bf16[1,24,3584]{2,1,0:T(8,128)(2,1)S(1)} %get-tuple-element.8), channel_id=1, source_target_pairs={{0,4},{2,6},{4,0},{6,2},{1,5},{3,7},{5,1},{7,3},{8,12},{10,14},{12... | collective-permute-start | bytes 516104 | tf_op jit(solution)/shard_map/ppermute | solution.py:72
  76.3 0.5 collective-permute-start.4
  76.8 2.8 %collective-permute-done.2 = bf16[1,24,3584]{2,1,0:T(8,128)(2,1)S(1)} collective-permute-done((bf16[1,24,3584]{2,1,0:T(8,128)(2,1)S(1)}, bf16[1,24,3584]{2,1,0:T(8,128)(2,1)S(1)}, u32[]{:S(2)}, u32[]{:S(2)}) %collective-permute-start.2) | collective-permute-done | bytes 172064 | tf_op jit(solution)/shard_map/ppermute | solution.py:72
  79.6 8.8 %collective-permute-done.3 = bf16[1,24,3584]{2,1,0:T(8,128)(2,1)S(1)} collective-permute-done((bf16[1,24,3584]{2,1,0:T(8,128)(2,1)S(1)}, bf16[1,24,3584]{2,1,0:T(8,128)(2,1)S(1)}, u32[]{:S(2)}, u32[]{:S(2)}) %collective-permute-start.3) | collective-permute-done | bytes 172064 | tf_op jit(solution)/shard_map/ppermute | solution.py:72
  88.5 0.8 gather_fusion.1
  89.3 0.2 reshape.121
  89.5 0.6 fusion.27
  90.1 0.7 fusion.14
  (24 shorter events, 0.2 us)
Async XLA Ops:
  6.5 42.7 %copy-start = (f32[1,3584,4]{1,2,0:T(4,128)S(1)}, f32[1,3584,4]{1,2,0:T(4,128)}, u32[]{:S(2)}) copy-start(f32[1,3584,4]{1,2,0:T(4,128)} %param.9) | copy-start | bytes 172036
  7.5 6.6 %collective-permute-start.1 = (bf16[1,16,3584]{2,1,0:T(8,128)(2,1)S(1)}, bf16[1,16,3584]{2,1,0:T(8,128)(2,1)S(1)}, u32[]{:S(2)}, u32[]{:S(2)}) collective-permute-start(bf16[1,16,3584]{2,1,0:T(8,128)(2,1)S(1)} %get-tuple-element.12), channel_id=1, source_target_pairs={{0,24},{8,0},{16,8},{24,16},{1,25},{9,1},{17,9},{25,17},{2,26},{10... | collective-permute-start | bytes 344072 | tf_op jit(solution)/shard_map/ppermute | solution.py:12
  10.0 4.6 %collective-permute-start = (bf16[1,16,3584]{2,1,0:T(8,128)(2,1)S(1)}, bf16[1,16,3584]{2,1,0:T(8,128)(2,1)S(1)}, u32[]{:S(2)}, u32[]{:S(2)}) collective-permute-start(bf16[1,16,3584]{2,1,0:T(8,128)(2,1)S(1)} %get-tuple-element.11), channel_id=1, source_target_pairs={{0,8},{8,16},{16,24},{24,0},{1,9},{9,17},{17,25},{25,1},{2,10},{10... | collective-permute-start | bytes 344072 | tf_op jit(solution)/shard_map/ppermute | solution.py:12
  21.6 22.2 %all-to-all-start = ((bf16[4,24,3584]{2,1,0:T(8,128)(2,1)}), bf16[4,24,3584]{2,1,0:T(8,128)(2,1)S(1)}, u32[]{:S(2)}, u32[]{:S(2)}) async-start(bf16[4,24,3584]{2,1,0:T(8,128)(2,1)} %bitcast.9), calls=%async_computation | async-start | bytes 1376256 | tf_op jit(solution)/shard_map/all_to_all | solution.py:54
  26.5 34.8 %reduce-scatter.2.cloned.1.call-start = ((), (), s32[]{:S(2)}) async-start(), calls=%async_computation.2 | async-start | bytes 589824 | tf_op jit(solution)/shard_map/reduce_scatter | solution.py:58
  43.8 5.2 %copy-start.1 = (s32[2,1,16,2]{2,3,1,0:T(2,128)S(1)}, s32[2,1,16,2]{2,3,1,0:T(2,128)}, u32[]{:S(2)}) copy-start(s32[2,1,16,2]{2,3,1,0:T(2,128)} %param.7) | copy-start | bytes 772
  72.1 7.4 %collective-permute-start.2 = (bf16[1,24,3584]{2,1,0:T(8,128)(2,1)S(1)}, bf16[1,24,3584]{2,1,0:T(8,128)(2,1)S(1)}, u32[]{:S(2)}, u32[]{:S(2)}) collective-permute-start(bf16[1,24,3584]{2,1,0:T(8,128)(2,1)S(1)} %get-tuple-element.9), channel_id=1, source_target_pairs={{0,2},{2,0},{4,6},{6,4},{1,3},{3,1},{5,7},{7,5},{8,10},{10,8},{12,... | collective-permute-start | bytes 516104 | tf_op jit(solution)/shard_map/ppermute | solution.py:72
  73.8 14.6 %collective-permute-start.3 = (bf16[1,24,3584]{2,1,0:T(8,128)(2,1)S(1)}, bf16[1,24,3584]{2,1,0:T(8,128)(2,1)S(1)}, u32[]{:S(2)}, u32[]{:S(2)}) collective-permute-start(bf16[1,24,3584]{2,1,0:T(8,128)(2,1)S(1)} %get-tuple-element.8), channel_id=1, source_target_pairs={{0,4},{2,6},{4,0},{6,2},{1,5},{3,7},{5,1},{7,3},{8,12},{10,14},{12... | collective-permute-start | bytes 516104 | tf_op jit(solution)/shard_map/ppermute | solution.py:72
  76.3 12.2 %collective-permute-start.4 = (bf16[1,24,3584]{2,1,0:T(8,128)(2,1)S(1)}, bf16[1,24,3584]{2,1,0:T(8,128)(2,1)S(1)}, u32[]{:S(2)}, u32[]{:S(2)}) collective-permute-start(bf16[1,24,3584]{2,1,0:T(8,128)(2,1)S(1)} %get-tuple-element.7), channel_id=1, source_target_pairs={{0,6},{2,4},{4,2},{6,0},{1,7},{3,5},{5,3},{7,1},{8,14},{10,12},{12... | collective-permute-start | bytes 516104 | tf_op jit(solution)/shard_map/ppermute | solution.py:72
Sparse Core Ops, SparseCore 0:
  49.1 12.2 reduce-scatter.1
